TPU v7x, 32 devices: a whole 2x2x4 slice. The times are simulated.
32 devices in a mesh: sec: 4 (over z), harm: 8 (over y, x, core).
Axes of the slice: x: 2, y: 2, z: 4, core: 2. Of those that a mesh axis runs over, the one named last changes fastest.
Arguments:
- displacement: bfloat16 [12, 64, 32, 48, 128], P('sec', 'harm'), may hold values from -3 to 3
- stiffness: bfloat16 [32, 1536, 1536], P('harm'), may hold values from -0.15625 to 0.15625
- contact_limit: float32 [12, 32, 48], P('sec', None, 'harm'), may hold values from 1 to 12
- pair_list: int32 [72, 3], replicated, may hold values from 0 to 31, as said below
- pair_count: int32 [4], replicated, may hold values from 3 to 18, as said below
Outputs:
- residual: bfloat16 [12, 64, 32, 48, 128], P('sec', 'harm')
Inputs may be any that keep to these rules, and one draw needn't show every extreme that they name: `pair_list`: rows of index i of sec (the aligned blocks of 18 rows) have owners among sectors i * 3 to i * 3 + 2 and partners equal to owner + 1 or owner - 1 modulo 12; rows at or past that index's pair_count are unused and hold entries in range; among used rows of one index, at most 6 have partners on the same index, at most 6 on index i + 1 and at most 6 on index i - 1 (modulo the size of sec), and some index reaches 6 in all three groups in every draw. `pair_count`: every index of sec has at least one used row in each of its three groups; some index uses all its rows.
All inputs are finite; a program needn't handle non-finite values.
Results may differ from a plain program's by a relative error of at most 0.004.
Values may be sent and summed in bfloat16 or wider, within the bound.
No kernel may reach another device: no remote copies, remote signals or barrier semaphores. Data moves between devices by JAX's collectives and lax.ppermute only.
A program may use at most 192 MiB of HBM per device.

v0:
```python
import math
import jax
import jax.numpy as jnp
from jax import lax
from jax.sharding import PartitionSpec as P

NT = 128


def with_halo(cells, sides, width):
    for axis, dim in sides:
        count = lax.axis_size(axis)
        head = lax.slice_in_dim(cells, 0, width, axis=dim)
        tail = lax.slice_in_dim(cells, cells.shape[dim] - width, cells.shape[dim], axis=dim)
        cells = jnp.concatenate(
            [
                lax.ppermute(tail, axis, [(i, (i + 1) % count) for i in range(count)]),
                cells,
                lax.ppermute(head, axis, [((i + 1) % count, i) for i in range(count)]),
            ],
            axis=dim,
        )
    return cells


def tables(sample_count, coeff_count):
    n_index = jnp.arange(sample_count, dtype=jnp.int32)[:, None]
    c_index = jnp.arange(coeff_count, dtype=jnp.int32)[None, :]
    harmonic = c_index // 2 + 1
    phases = (harmonic * n_index % sample_count).astype(jnp.float32) * (
        2.0 * math.pi / sample_count
    )
    waveform = jnp.where(c_index % 2 == 0, jnp.cos(phases), jnp.sin(phases))
    return (waveform.astype(jnp.bfloat16), (waveform * (2.0 / sample_count)).astype(jnp.bfloat16))


def on_device(displacement, stiffness, contact_limit, pair_list, pair_count):
    sec_count = lax.axis_size("sec")
    sec_index = lax.axis_index("sec")
    harm_count = lax.axis_size("harm")
    sectors_here, coeffs_here, blocks_total, dofs_total, batch_cols = displacement.shape
    coeff_total = coeffs_here * harm_count
    forward_table, inverse_table = tables(NT, coeff_total)
    exchanged = lax.all_to_all(displacement, "harm", split_axis=3, concat_axis=1, tiled=True)
    waveform = jnp.einsum(
        "nc,scbdx->snbdx", forward_table, exchanged, preferred_element_type=jnp.float32
    )
    samples = waveform.astype(jnp.bfloat16)
    slots_dev = pair_list.shape[0] // sec_count
    capacity = slots_dev // 3
    sector_total = sectors_here * sec_count

    def bucket(device):
        rows = lax.dynamic_slice_in_dim(pair_list, device * slots_dev, slots_dev, 0)
        row_index = jnp.arange(slots_dev, dtype=jnp.int32)
        is_valid = row_index < pair_count[device]
        owners = rows[:, 0]
        partners = rows[:, 1]
        blocks = rows[:, 2]
        partner_dev = partners // sectors_here
        group = jnp.where(
            partner_dev == device, 0, jnp.where(partners == (owners + 1) % sector_total, 1, 2)
        )
        matches = (
            (group[:, None] == jnp.arange(3, dtype=jnp.int32)[None, :]) & is_valid[:, None]
        ).astype(jnp.int32)
        before = jnp.cumsum(matches, axis=0) - matches
        ranking = jnp.sum(before * matches, axis=1)
        slot_index = jnp.where(is_valid, group * capacity + ranking, slots_dev)
        source = jnp.zeros((slots_dev,), jnp.int32).at[slot_index].set(row_index, mode="drop")
        live = jnp.zeros((slots_dev,), jnp.int32).at[slot_index].set(1, mode="drop")
        return (
            owners[source] - device * sectors_here,
            partners[source] - partner_dev[source] * sectors_here,
            blocks[source],
            live > 0,
        )

    own_owner, own_partner, own_block, own_live = bucket(sec_index)
    prev_bucket = bucket((sec_index + sec_count - 1) % sec_count)
    next_bucket = bucket((sec_index + 1) % sec_count)
    send_order = jnp.concatenate(
        [
            jnp.arange(2 * capacity, 3 * capacity, dtype=jnp.int32),
            jnp.arange(capacity, 2 * capacity, dtype=jnp.int32),
        ]
    )
    send_owner = own_owner[send_order]
    send_block = own_block[send_order]
    send_live = own_live[send_order]
    outgoing = samples[send_owner, :, send_block]
    outgoing = jnp.where(send_live[:, None, None, None], outgoing, jnp.zeros_like(outgoing))
    padded = with_halo(outgoing.reshape((2, capacity) + outgoing.shape[1:]), (("sec", 0),), 1)
    remote_wave = jnp.concatenate([padded[0], padded[3]], axis=0)
    local_wave = samples[own_owner[:capacity], :, own_block[:capacity]]
    owner_wave = jnp.concatenate([local_wave, remote_wave], axis=0)
    partner_index = jnp.concatenate(
        [
            own_partner[:capacity],
            prev_bucket[1][capacity : 2 * capacity],
            next_bucket[1][2 * capacity :],
        ]
    )
    block_index = jnp.concatenate(
        [
            own_block[:capacity],
            prev_bucket[2][capacity : 2 * capacity],
            next_bucket[2][2 * capacity :],
        ]
    )
    live_rows = jnp.concatenate(
        [
            own_live[:capacity],
            prev_bucket[3][capacity : 2 * capacity],
            next_bucket[3][2 * capacity :],
        ]
    )
    partner_wave = samples[partner_index, :, block_index]
    limits = contact_limit[partner_index, block_index][:, None, :, None]
    relative = owner_wave.astype(jnp.float32) - partner_wave.astype(jnp.float32)
    friction = jnp.where(
        live_rows[:, None, None, None], limits * jnp.tanh(relative / limits), jnp.float32(0.0)
    ).astype(jnp.bfloat16)
    pair_coeffs = jnp.einsum(
        "nc,rndx->rcdx", inverse_table, friction, preferred_element_type=jnp.float32
    ).astype(jnp.bfloat16)
    force = jnp.zeros(
        (sectors_here, coeff_total, blocks_total, samples.shape[3], batch_cols), jnp.float32
    )
    force = force.at[partner_index, :, block_index].add(-pair_coeffs.astype(jnp.float32))
    force = force.at[own_owner[:capacity], :, own_block[:capacity]].add(
        pair_coeffs[:capacity].astype(jnp.float32)
    )
    remote_force = friction[capacity:]
    back = with_halo(remote_force.reshape((2, capacity) + remote_force.shape[1:]), (("sec", 0),), 1)
    returned_wave = jnp.concatenate([back[3], back[0]], axis=0)
    returned = jnp.einsum(
        "nc,rndx->rcdx", inverse_table, returned_wave, preferred_element_type=jnp.float32
    ).astype(jnp.bfloat16)
    force = force.at[own_owner[capacity:], :, own_block[capacity:]].add(
        returned.astype(jnp.float32)
    )
    force_coeffs = force.astype(jnp.bfloat16)
    returned_coeffs = lax.all_to_all(force_coeffs, "harm", split_axis=1, concat_axis=3, tiled=True)
    harmonics_here = stiffness.shape[0]
    paired = displacement.reshape(
        sectors_here, harmonics_here, 2, blocks_total * dofs_total, batch_cols
    )
    product = jnp.einsum("hij,shpjx->shpix", stiffness, paired, preferred_element_type=jnp.float32)
    result = product.reshape(displacement.shape) + returned_coeffs.astype(jnp.float32)
    return result.astype(jnp.bfloat16)


def solution(mesh):
    in_specs = (
        P("sec", "harm", None, None, None),
        P("harm", None, None),
        P("sec", None, "harm"),
        P(),
        P(),
    )
    out_specs = P("sec", "harm", None, None, None)
    return jax.shard_map(
        on_device, mesh=mesh, in_specs=in_specs, out_specs=out_specs, check_vma=False
    )
```

profile of v0, /device:TPU:0, one launch (start us, length us, event | category | flops | bytes accessed | tf_op | source)
XLA Modules:
  0.0 445.1 jit_solution(13424681273661140205)
XLA Ops:
  0.0 9.9 %copy.38 = bf16[3,8,32,48,128]{4,2,1,0,3:T(8,128)(2,1)} copy(bf16[3,8,32,48,128]{4,3,2,1,0:T(8,128)(2,1)} %param.5) | data formatting | bytes 18874368 | tf_op args[0]
  9.9 5.3 %all-to-all-start = ((bf16[3,8,32,48,128]{4,2,1,0,3:T(8,128)(2,1)}), bf16[3,8,32,48,128]{4,2,1,0,3:T(8,128)(2,1)}, u32[]{:S(2)}, u32[]{:S(2)}) async-start(bf16[3,8,32,48,128]{4,2,1,0,3:T(8,128)(2,1)} %copy.38), calls=%async_computation | async-start | bytes 18874368 | tf_op jit(solution)/shard_map/all_to_all | solution.py:44
  15.3 0.7 fusion.88
  21.7 0.7 iota_compare_fusion.5
  22.7 0.7 fusion.57
  24.8 0.7 gather_fusion.5
  25.5 0.7 gather_fusion.4
  26.2 0.7 gather_fusion.3
  26.9 0.7 gather_fusion.2
  27.6 0.7 gather_fusion.1
  28.3 0.7 gather_fusion
  29.0 0.7 gather_fusion.6
  29.7 0.7 gather_fusion.10
  31.9 0.7 gather_fusion.12
  32.7 88.4 %all-to-all-done = bf16[3,8,32,48,128]{4,2,1,0,3:T(8,128)(2,1)} async-done(((bf16[3,8,32,48,128]{4,2,1,0,3:T(8,128)(2,1)}), bf16[3,8,32,48,128]{4,2,1,0,3:T(8,128)(2,1)}, u32[]{:S(2)}, u32[]{:S(2)}) %all-to-all-start) | async-done | bytes 9437216 | tf_op jit(solution)/shard_map/all_to_all | solution.py:44
  121.1 12.1 %convert_bitcast_fusion.1 = bf16[3,128,32,6,128]{4,1,3,2,0:T(8,128)(2,1)} fusion(bf16[3,8,8,32,6,128]{5,3,2,0,4,1:T(8,128)(2,1)} %bitcast.35, s32[64]{0:T(128)S(1)} %fusion.44, pred[64]{0:T(512)(128)(4,1)S(1)} %fusion.43), kind=kOutput, calls=%fused_computation.31 | convolution fusion | flops 1217527808 | bytes 28311872 | tf_op jit(solution)/shard_map/nc,scbdx->snbdx/dot_general | solution.py:45
  133.2 7.4 %gather_fusion.15 = bf16[12,128,6,128]{3,1,2,0:T(8,128)(2,1)S(1)} fusion(bf16[3,128,32,6,128]{4,1,3,2,0:T(8,128)(2,1)} %convert_bitcast_fusion.1, s32[12]{0:T(128)S(1)} %fusion.55), kind=kCustom, calls=%fused_computation.15 | custom fusion | bytes 4718688 | tf_op jit(solution)/shard_map/gather | solution.py:91
  140.9 1.6 slice_bitcast_fusion.3
  142.5 2.4 collective-permute-start
  144.8 2.3 collective-permute-start.1
  147.2 0.7 gather_fusion.8
  147.9 0.7 gather_fusion.7
  149.7 1.4 gather_fusion.9
  152.3 7.8 %gather_fusion.16 = bf16[18,128,6,128]{3,1,2,0:T(8,128)(2,1)S(1)} fusion(bf16[3,128,32,6,128]{4,1,3,2,0:T(8,128)(2,1)} %convert_bitcast_fusion.1, s32[18]{0:T(128)S(1)} %get-tuple-element.5), kind=kCustom, calls=%fused_computation.16 | custom fusion | bytes 7078032 | tf_op jit(solution)/shard_map/gather | solution.py:118
  160.0 8.2 %gather_fusion.11 = bf16[6,128,6,128]{3,1,2,0:T(8,128)(2,1)} fusion(bf16[3,128,32,6,128]{4,1,3,2,0:T(8,128)(2,1)} %convert_bitcast_fusion.1, s32[6]{0:T(128)S(1)} %get-tuple-element.26), kind=kCustom, calls=%fused_computation.11 | custom fusion | bytes 2359344 | tf_op jit(solution)/shard_map/gather | solution.py:95
  168.2 5.8 %collective-permute-done = bf16[1,6,128,6,128]{4,2,3,1,0:T(8,128)(2,1)} collective-permute-done((bf16[1,6,128,6,128]{4,2,3,1,0:T(8,128)(2,1)}, bf16[1,6,128,6,128]{4,2,3,1,0:T(8,128)(2,1)}, u32[]{:S(2)}, u32[]{:S(2)}) %collective-permute-start) | collective-permute-done | bytes 1179680 | tf_op jit(solution)/shard_map/ppermute | solution.py:17
  174.0 21.1 %collective-permute-done.1 = bf16[1,6,128,6,128]{4,2,3,1,0:T(8,128)(2,1)} collective-permute-done((bf16[1,6,128,6,128]{4,2,3,1,0:T(8,128)(2,1)}, bf16[1,6,128,6,128]{4,2,3,1,0:T(8,128)(2,1)}, u32[]{:S(2)}, u32[]{:S(2)}) %collective-permute-start.1) | collective-permute-done | bytes 1179680 | tf_op jit(solution)/shard_map/ppermute | solution.py:19
  195.2 4.0 select_convert_fusion
  199.2 1.7 slice_bitcast_fusion.1
  201.0 2.1 collective-permute-start.2
  203.2 2.0 convert_negate_fusion
  205.2 8.9 %broadcast_in_dim.72 = f32[3,64,32,6,128]{4,1,3,2,0:T(8,128)} broadcast(f32[]{:T(128)} %constant.120.clone.1), dimensions={} | broadcast | bytes 18874372 | tf_op jit(solution)/shard_map/broadcast_in_dim | solution.py:127
  214.1 10.9 %scatter_fusion = f32[3,64,32,6,128]{4,1,3,2,0:T(8,128)} fusion(f32[3,64,32,6,128]{4,1,3,2,0:T(8,128)} %broadcast_in_dim.72, s32[18]{0:T(128)S(1)} %fusion.60, f32[18,64,6,128]{3,1,2,0:T(8,128)S(1)} %get-tuple-element.30), kind=kCustom, calls=%fused_computation.23 | custom fusion | flops 884736 | bytes 10616976 | tf_op jit(solution)/shard_map/scatter-add | solution.py:130
  224.9 1.2 slice_convert_fusion
  226.1 3.6 scatter_fusion.1
  229.8 24.3 %collective-permute-done.2 = bf16[1,6,128,6,128]{4,2,3,1,0:T(8,128)(2,1)} collective-permute-done((bf16[1,6,128,6,128]{4,2,3,1,0:T(8,128)(2,1)}, bf16[1,6,128,6,128]{4,2,3,1,0:T(8,128)(2,1)}, u32[]{:S(2)}, u32[]{:S(2)}) %collective-permute-start.2) | collective-permute-done | bytes 1179680 | tf_op jit(solution)/shard_map/ppermute | solution.py:19
  254.1 2.3 convert_bitcast_fusion.2
  256.4 7.0 %scatter_fusion.2 = f32[3,64,32,6,128]{4,1,3,2,0:T(8,128)} fusion(f32[3,64,32,6,128]{4,1,3,2,0:T(8,128)} %scatter_fusion.1, s32[12]{0:T(128)S(1)} %fusion.56, f32[12,64,6,128]{3,1,2,0:T(8,128)S(1)} %convert_bitcast_fusion.2), kind=kCustom, calls=%fused_computation.25 | custom fusion | flops 589824 | bytes 7077984 | tf_op jit(solution)/shard_map/scatter-add | solution.py:140
  263.4 10.4 %convert_element_type.97 = bf16[3,64,32,6,128]{4,1,3,2,0:T(8,128)(2,1)} convert(f32[3,64,32,6,128]{4,1,3,2,0:T(8,128)} %scatter_fusion.2) | non-fusion elementwise | flops 4718592 | bytes 28311552 | tf_op jit(solution)/shard_map/convert_element_type | solution.py:143
  273.8 13.3 %copy.41 = bf16[3,64,32,6,128]{4,2,3,0,1:T(8,128)(2,1)} copy(bf16[3,64,32,6,128]{4,1,3,2,0:T(8,128)(2,1)} %convert_element_type.97) | data formatting | bytes 18874368 | tf_op jit(solution)/shard_map/convert_element_type | solution.py:143
  287.1 5.4 %all-to-all-start.1 = ((bf16[3,64,32,6,128]{4,2,3,0,1:T(8,128)(2,1)}), bf16[3,64,32,6,128]{4,2,3,0,1:T(8,128)(2,1)}, u32[]{:S(2)}, u32[]{:S(2)}) async-start(bf16[3,64,32,6,128]{4,2,3,0,1:T(8,128)(2,1)} %copy.41), calls=%async_computation.1 | async-start | bytes 18874368 | tf_op jit(solution)/shard_map/all_to_all | solution.py:144
  292.5 25.0 %fusion.6 = f32[3,4,2,1536,128]{3,4,2,0,1:T(8,128)} fusion(bf16[4,1536,1536]{2,1,0:T(8,128)(2,1)} %param.6, bf16[3,4,2,1536,128]{4,3,2,1,0:T(8,128)(2,1)} %bitcast.179), kind=kOutput, calls=%fused_computation.35 | convolution fusion | flops 14495514624 | bytes 47185920 | tf_op jit(solution)/shard_map/hij,shpjx->shpix/dot_general | solution.py:149
  317.4 18.6 %copy.36 = f32[3,4,2,1536,128]{4,3,2,1,0:T(8,128)} copy(f32[3,4,2,1536,128]{3,4,2,0,1:T(8,128)} %fusion.6) | data formatting | bytes 37748736 | tf_op jit(solution)/shard_map/hij,shpjx->shpix/transpose | solution.py:149
  336.1 61.7 %all-to-all-done.1 = bf16[3,64,32,6,128]{4,2,3,0,1:T(8,128)(2,1)} async-done(((bf16[3,64,32,6,128]{4,2,3,0,1:T(8,128)(2,1)}), bf16[3,64,32,6,128]{4,2,3,0,1:T(8,128)(2,1)}, u32[]{:S(2)}, u32[]{:S(2)}) %all-to-all-start.1) | async-done | bytes 9437216 | tf_op jit(solution)/shard_map/all_to_all | solution.py:144
  397.8 10.1 %copy.42 = bf16[3,64,32,6,128]{4,2,3,1,0:T(8,128)(2,1)} copy(bf16[3,64,32,6,128]{4,2,3,0,1:T(8,128)(2,1)} %all-to-all-done.1) | data formatting | bytes 18874368 | tf_op jit(solution)/shard_map/all_to_all | solution.py:144
  407.9 12.9 %convert_bitcast_fusion = f32[3,8,32,8,6,128]{5,2,4,1,3,0:T(8,128)} fusion(bf16[3,8,8,32,6,128]{5,3,4,2,1,0:T(8,128)(2,1)} %bitcast.178), kind=kLoop, calls=%fused_computation.26 | loop fusion | flops 4718592 | bytes 28311552 | tf_op jit(solution)/shard_map/convert_element_type | solution.py:150
  420.7 8.2 %copy.43 = f32[3,8,32,8,6,128]{5,2,4,3,1,0:T(8,128)S(1)} copy(f32[3,8,32,8,6,128]{5,2,4,1,3,0:T(8,128)} %convert_bitcast_fusion) | data formatting | bytes 37748736 | tf_op jit(solution)/shard_map/convert_element_type | solution.py:150
  428.9 15.9 %fusion.2 = bf16[3,8,32,48,128]{4,3,2,1,0:T(8,128)(2,1)} fusion(f32[3,8,32,48,128]{4,3,2,1,0:T(8,128)} %bitcast.176, f32[3,8,32,48,128]{4,2,3,1,0:T(8,128)S(1)} %bitcast.177), kind=kLoop, calls=%fused_computation.30 | loop fusion | flops 9437184 | bytes 47185920 | tf_op jit(solution)/shard_map/convert_element_type | solution.py:151
  (86 shorter events, 11.5 us)
Async XLA Ops:
  9.9 5.3 %copy-start.8 = (s32[4]{0:T(128)S(1)}, s32[4]{0:T(128)}, u32[]{:S(2)}) copy-start(s32[4]{0:T(128)} %param.9) | copy-start | bytes 52
  9.9 6.7 %copy-start.1 = (s32[72,3]{0,1:T(4,128)S(1)}, s32[72,3]{0,1:T(4,128)}, u32[]{:S(2)}) copy-start(s32[72,3]{0,1:T(4,128)} %param.8) | copy-start | bytes 2596
  9.9 111.2 %all-to-all-start = ((bf16[3,8,32,48,128]{4,2,1,0,3:T(8,128)(2,1)}), bf16[3,8,32,48,128]{4,2,1,0,3:T(8,128)(2,1)}, u32[]{:S(2)}, u32[]{:S(2)}) async-start(bf16[3,8,32,48,128]{4,2,1,0,3:T(8,128)(2,1)} %copy.38), calls=%async_computation | async-start | bytes 18874368 | tf_op jit(solution)/shard_map/all_to_all | solution.py:44
  32.5 88.6 %copy-start.3 = (pred[64]{0:T(512)(128)(4,1)}, pred[64]{0:T(512)(128)(4,1)S(1)}, u32[]{:S(2)}) copy-start(pred[64]{0:T(512)(128)(4,1)S(1)} %fusion.43) | copy-start | bytes 196
  32.6 88.5 %copy-start.5 = (s32[64]{0:T(128)}, s32[64]{0:T(128)S(1)}, u32[]{:S(2)}) copy-start(s32[64]{0:T(128)S(1)} %fusion.44) | copy-start | bytes 772
  140.9 7.8 %copy-start.2 = (f32[3,32,6]{1,2,0:T(8,128)S(1)}, f32[3,32,6]{1,2,0:T(8,128)}, u32[]{:S(2)}) copy-start(f32[3,32,6]{1,2,0:T(8,128)} %param.7) | copy-start | bytes 6916
  142.5 31.6 %collective-permute-start = (bf16[1,6,128,6,128]{4,2,3,1,0:T(8,128)(2,1)}, bf16[1,6,128,6,128]{4,2,3,1,0:T(8,128)(2,1)}, u32[]{:S(2)}, u32[]{:S(2)}) collective-permute-start(bf16[1,6,128,6,128]{4,2,3,1,0:T(8,128)(2,1)} %get-tuple-element.10), channel_id=1, source_target_pairs={{0,8},{8,16},{16,24},{24,0},{1,9},{9,17},{17,25},{25,1},{2,10},{10... | collective-permute-start | bytes 3538952 | tf_op jit(solution)/shard_map/ppermute | solution.py:17
  144.8 50.3 %collective-permute-start.1 = (bf16[1,6,128,6,128]{4,2,3,1,0:T(8,128)(2,1)}, bf16[1,6,128,6,128]{4,2,3,1,0:T(8,128)(2,1)}, u32[]{:S(2)}, u32[]{:S(2)}) collective-permute-start(bf16[1,6,128,6,128]{4,2,3,1,0:T(8,128)(2,1)} %get-tuple-element.11), channel_id=1, source_target_pairs={{8,0},{16,8},{24,16},{0,24},{9,1},{17,9},{25,17},{1,25},{10,2},{18... | collective-permute-start | bytes 3538952 | tf_op jit(solution)/shard_map/ppermute | solution.py:19
  199.2 3.9 copy-start.9
  199.2 3.9 copy-start.10
  199.2 3.9 copy-start.4
  199.2 3.9 copy-start.6
  201.0 53.2 %collective-permute-start.2 = (bf16[1,6,128,6,128]{4,2,3,1,0:T(8,128)(2,1)}, bf16[1,6,128,6,128]{4,2,3,1,0:T(8,128)(2,1)}, u32[]{:S(2)}, u32[]{:S(2)}) collective-permute-start(bf16[1,6,128,6,128]{4,2,3,1,0:T(8,128)(2,1)} %get-tuple-element.8), channel_id=1, source_target_pairs={{8,0},{16,8},{24,16},{0,24},{9,1},{17,9},{25,17},{1,25},{10,2},{18... | collective-permute-start | bytes 3538952 | tf_op jit(solution)/shard_map/ppermute | solution.py:19
  203.0 51.1 %collective-permute-start.3 = (bf16[1,6,128,6,128]{4,2,3,1,0:T(8,128)(2,1)}, bf16[1,6,128,6,128]{4,2,3,1,0:T(8,128)(2,1)}, u32[]{:S(2)}, u32[]{:S(2)}) collective-permute-start(bf16[1,6,128,6,128]{4,2,3,1,0:T(8,128)(2,1)} %get-tuple-element.9), channel_id=1, source_target_pairs={{0,8},{8,16},{16,24},{24,0},{1,9},{9,17},{17,25},{25,1},{2,10},{10... | collective-permute-start | bytes 3538952 | tf_op jit(solution)/shard_map/ppermute | solution.py:17
  214.1 12.1 %copy-start = (s32[6]{0:T(128)S(1)}, s32[6]{0:T(128)}, u32[]{:S(2)}) copy-start(s32[6]{0:T(128)} %get-tuple-element.25) | copy-start | bytes 76
  224.9 29.2 %copy-start.7 = (s32[64]{0:T(128)S(1)}, s32[64]{0:T(128)}, u32[]{:S(2)}) copy-start(s32[64]{0:T(128)} %copy-done.5) | copy-start | bytes 772
  287.1 110.7 %all-to-all-start.1 = ((bf16[3,64,32,6,128]{4,2,3,0,1:T(8,128)(2,1)}), bf16[3,64,32,6,128]{4,2,3,0,1:T(8,128)(2,1)}, u32[]{:S(2)}, u32[]{:S(2)}) async-start(bf16[3,64,32,6,128]{4,2,3,0,1:T(8,128)(2,1)} %copy.41), calls=%async_computation.1 | async-start | bytes 18874368 | tf_op jit(solution)/shard_map/all_to_all | solution.py:144
where the time goes:
time: 453 us; the launch traced here: 445 us
  waiting for transfers between devices  201 us (44%)
  local copies, waits for them, and re-layouts  111 us (25%)
  other arithmetic  73 us (16%)
  matrix products  41.4 us (9%)
  starting transfers between devices  17.5 us (4%)
    all_to_all x1, waiting for transfers between devices, on_device(): lax.all_to_all(displacement, 'harm', split_axis=3, concat_axis=1, tiled=T...  88.4 us
    all_to_all x1, waiting for transfers between devices, on_device(): lax.all_to_all(force_coeffs, 'harm', split_axis=1, concat_axis=3, tiled=T...  61.7 us
    ppermute x2, waiting for transfers between devices, with_halo(): lax.ppermute(head, axis, [((i + 1) % count, i) for i in range(count)])  45.5 us
    dot_general x1, matrix products, on_device(): jnp.einsum('hij,shpjx->shpix', stiffness, paired, preferred_element_type=...  25 us
    transpose x1, local copies, waits for them, and re-layouts, on_device(): jnp.einsum('hij,shpjx->shpix', stiffness, paired, preferred_element_type=...  18.6 us
    convert_element_type x1, other arithmetic, on_device(): return result.astype(jnp.bfloat16)  15.9 us
    convert_element_type x1, local copies, waits for them, and re-layouts, on_device(): force_coeffs = force.astype(jnp.bfloat16)  13.3 us
    convert_element_type x1, other arithmetic, on_device(): returned_coeffs.astype(jnp.float32)  12.9 us
  transfers between devices with their start and end apart: 6, of which 5 were waited for; matrix products, arithmetic and copies ran while one was open for 24% of the time, Pallas kernels for 0%

commit v1 on v0

--- a/solution.py
+++ b/solution.py
@@ -141,7 +141,11 @@
         returned.astype(jnp.float32)
     )
     force_coeffs = force.astype(jnp.bfloat16)
-    returned_coeffs = lax.all_to_all(force_coeffs, "harm", split_axis=1, concat_axis=3, tiled=True)
+    axis_part_render = lambda unit: jnp.concatenate(
+        lax.all_to_all(jnp.stack(jnp.split(unit, lax.axis_size("harm"), axis=1), 0), "harm", 0, 0),
+        3,
+    )
+    returned_coeffs = axis_part_render(force_coeffs)
     harmonics_here = stiffness.shape[0]
     paired = displacement.reshape(
         sectors_here, harmonics_here, 2, blocks_total * dofs_total, batch_cols

time: 453 us -> 432 us (0.954); the launches traced: 445 us -> 431 us
  local copies, waits for them, and re-layouts: 111 us -> 103 us
  other arithmetic: 73 us -> 66.4 us
    ppermute x2, waiting for transfers between devices: 5.82 us -> 29.5 us  [with_halo(): lax.ppermute(tail, axis, [(i, (i + 1) % count) for i in range(count)])]
    ppermute x2, waiting for transfers between devices: 45.5 us -> 22 us  [with_halo(): lax.ppermute(head, axis, [((i + 1) % count, i) for i in range(count)])]
    convert_element_type x1 -> x0, local copies, waits for them, and re-layouts: 13.3 us -> none  [on_device(): force_coeffs = force.astype(jnp.bfloat16)]
    all_to_all x1 -> x0, local copies, waits for them, and re-layouts: 10.1 us -> none  [on_device(): lax.all_to_all(force_coeffs, 'harm', split_axis=1, concat_axis=3, tiled=T...]
    unnamed x24 -> x33, local copies, waits for them, and re-layouts: 10.1 us -> 19.4 us
    convert_element_type x1, local copies, waits for them, and re-layouts: 8.18 us -> 12.8 us  [on_device(): returned_coeffs.astype(jnp.float32)]
  transfers between devices with their start and end apart: 6 -> 6, of which waited for: 5 -> 6; matrix products, arithmetic and copies ran while one was open for 24% -> 25% of each run, Pallas kernels for 0% -> 0%
where the time goes in v1:
time: 432 us; the launch traced here: 431 us
  waiting for transfers between devices  202 us (47%)
  local copies, waits for them, and re-layouts  103 us (24%)
  other arithmetic  66.4 us (15%)
  matrix products  41.4 us (10%)
  starting transfers between devices  17.5 us (4%)
    all_to_all x1, waiting for transfers between devices, on_device(): lax.all_to_all(displacement, 'harm', split_axis=3, concat_axis=1, tiled=T...  88.4 us
    all_to_all x1, waiting for transfers between devices, on_device(): lax.all_to_all(jnp.stack(jnp.split(unit, lax.axis_size('harm'), axis=1),...  61.8 us
    ppermute x2, waiting for transfers between devices, with_halo(): lax.ppermute(tail, axis, [(i, (i + 1) % count) for i in range(count)])  29.5 us
    dot_general x1, matrix products, on_device(): jnp.einsum('hij,shpjx->shpix', stiffness, paired, preferred_element_type=...  25 us
    ppermute x2, waiting for transfers between devices, with_halo(): lax.ppermute(head, axis, [((i + 1) % count, i) for i in range(count)])  22 us
    unnamed x33, local copies, waits for them, and re-layouts  19.4 us
    transpose x1, local copies, waits for them, and re-layouts, on_device(): jnp.einsum('hij,shpjx->shpix', stiffness, paired, preferred_element_type=...  18.6 us
    convert_element_type x1, other arithmetic, on_device(): return result.astype(jnp.bfloat16)  13.1 us
  transfers between devices with their start and end apart: 6, of which 6 were waited for; matrix products, arithmetic and copies ran while one was open for 25% of the time, Pallas kernels for 0%

profile of v1, /device:TPU:0, one launch (start us, length us, event | category | flops | bytes accessed | tf_op | source)
XLA Modules:
  0.0 430.5 jit_solution(8961034495386462939)
XLA Ops:
  0.0 9.9 %copy.19 = bf16[3,8,32,48,128]{4,2,1,0,3:T(8,128)(2,1)} copy(bf16[3,8,32,48,128]{4,3,2,1,0:T(8,128)(2,1)} %param.5) | data formatting | bytes 18874368 | tf_op args[0]
  9.9 5.3 %all-to-all-start = ((bf16[3,8,32,48,128]{4,2,1,0,3:T(8,128)(2,1)}), bf16[3,8,32,48,128]{4,2,1,0,3:T(8,128)(2,1)}, u32[]{:S(2)}, u32[]{:S(2)}) async-start(bf16[3,8,32,48,128]{4,2,1,0,3:T(8,128)(2,1)} %copy.19), calls=%async_computation | async-start | bytes 18874368 | tf_op jit(solution)/shard_map/all_to_all | solution.py:44
  25.5 0.7 gather_fusion.4
  26.9 0.7 gather_fusion.2
  27.6 0.7 gather_fusion.1
  28.3 0.7 gather_fusion
  29.0 0.7 gather_fusion.6
  29.7 0.7 gather_fusion.10
  32.7 88.4 %all-to-all-done = bf16[3,8,32,48,128]{4,2,1,0,3:T(8,128)(2,1)} async-done(((bf16[3,8,32,48,128]{4,2,1,0,3:T(8,128)(2,1)}), bf16[3,8,32,48,128]{4,2,1,0,3:T(8,128)(2,1)}, u32[]{:S(2)}, u32[]{:S(2)}) %all-to-all-start) | async-done | bytes 9437216 | tf_op jit(solution)/shard_map/all_to_all | solution.py:44
  121.1 12.1 %convert_bitcast_fusion.1 = bf16[3,128,32,6,128]{4,1,3,2,0:T(8,128)(2,1)} fusion(bf16[3,8,8,32,6,128]{5,3,2,0,4,1:T(8,128)(2,1)} %bitcast.35, s32[64]{0:T(128)S(1)} %fusion.52, pred[64]{0:T(512)(128)(4,1)S(1)} %fusion.51), kind=kOutput, calls=%fused_computation.31 | convolution fusion | flops 1217527808 | bytes 28311872 | tf_op jit(solution)/shard_map/nc,scbdx->snbdx/dot_general | solution.py:45
  133.2 7.4 %gather_fusion.15 = bf16[12,128,6,128]{3,1,2,0:T(8,128)(2,1)S(1)} fusion(bf16[3,128,32,6,128]{4,1,3,2,0:T(8,128)(2,1)} %convert_bitcast_fusion.1, s32[12]{0:T(128)S(1)} %fusion.63), kind=kCustom, calls=%fused_computation.15 | custom fusion | bytes 4718688 | tf_op jit(solution)/shard_map/gather | solution.py:91
  140.9 1.6 slice_bitcast_fusion.11
  142.5 2.4 collective-permute-start
  144.8 2.1 collective-permute-start.1
  147.7 0.7 gather_fusion.7
  149.4 1.4 gather_fusion.9
  152.0 7.8 %gather_fusion.16 = bf16[18,128,6,128]{3,1,2,0:T(8,128)(2,1)S(1)} fusion(bf16[3,128,32,6,128]{4,1,3,2,0:T(8,128)(2,1)} %convert_bitcast_fusion.1, s32[18]{0:T(128)S(1)} %get-tuple-element.5), kind=kCustom, calls=%fused_computation.16 | custom fusion | bytes 7078032 | tf_op jit(solution)/shard_map/gather | solution.py:118
  159.8 8.2 %gather_fusion.11 = bf16[6,128,6,128]{3,1,2,0:T(8,128)(2,1)} fusion(bf16[3,128,32,6,128]{4,1,3,2,0:T(8,128)(2,1)} %convert_bitcast_fusion.1, s32[6]{0:T(128)S(1)} %get-tuple-element.26), kind=kCustom, calls=%fused_computation.11 | custom fusion | bytes 2359344 | tf_op jit(solution)/shard_map/gather | solution.py:95
  167.9 6.1 %collective-permute-done = bf16[1,6,128,6,128]{4,2,3,1,0:T(8,128)(2,1)} collective-permute-done((bf16[1,6,128,6,128]{4,2,3,1,0:T(8,128)(2,1)}, bf16[1,6,128,6,128]{4,2,3,1,0:T(8,128)(2,1)}, u32[]{:S(2)}, u32[]{:S(2)}) %collective-permute-start) | collective-permute-done | bytes 1179680 | tf_op jit(solution)/shard_map/ppermute | solution.py:17
  174.0 20.9 %collective-permute-done.1 = bf16[1,6,128,6,128]{4,2,3,1,0:T(8,128)(2,1)} collective-permute-done((bf16[1,6,128,6,128]{4,2,3,1,0:T(8,128)(2,1)}, bf16[1,6,128,6,128]{4,2,3,1,0:T(8,128)(2,1)}, u32[]{:S(2)}, u32[]{:S(2)}) %collective-permute-start.1) | collective-permute-done | bytes 1179680 | tf_op jit(solution)/shard_map/ppermute | solution.py:19
  194.9 4.0 select_convert_fusion
  199.0 1.7 slice_bitcast_fusion.9
  200.7 2.3 collective-permute-start.2
  203.2 2.0 convert_negate_fusion
  205.2 8.9 %broadcast_in_dim.72 = f32[3,64,32,6,128]{4,1,3,2,0:T(8,128)} broadcast(f32[]{:T(128)} %constant.120.clone.1), dimensions={} | broadcast | bytes 18874372 | tf_op jit(solution)/shard_map/broadcast_in_dim | solution.py:127
  214.1 10.3 %scatter_fusion = f32[3,64,32,6,128]{4,1,3,2,0:T(8,128)} fusion(f32[3,64,32,6,128]{4,1,3,2,0:T(8,128)} %broadcast_in_dim.72, s32[18]{0:T(128)S(1)} %fusion.68, f32[18,64,6,128]{3,1,2,0:T(8,128)S(1)} %get-tuple-element.30), kind=kCustom, calls=%fused_computation.23 | custom fusion | flops 884736 | bytes 10616976 | tf_op jit(solution)/shard_map/scatter-add | solution.py:130
  224.4 1.2 slice_convert_fusion
  225.6 3.6 scatter_fusion.1
  229.3 1.1 collective-permute-done.2
  230.4 23.4 %collective-permute-done.3 = bf16[1,6,128,6,128]{4,2,3,1,0:T(8,128)(2,1)} collective-permute-done((bf16[1,6,128,6,128]{4,2,3,1,0:T(8,128)(2,1)}, bf16[1,6,128,6,128]{4,2,3,1,0:T(8,128)(2,1)}, u32[]{:S(2)}, u32[]{:S(2)}) %collective-permute-start.3) | collective-permute-done | bytes 1179680 | tf_op jit(solution)/shard_map/ppermute | solution.py:17
  253.8 2.3 convert_bitcast_fusion.2
  256.1 7.0 %scatter_fusion.2 = f32[3,64,32,6,128]{4,1,3,2,0:T(8,128)} fusion(f32[3,64,32,6,128]{4,1,3,2,0:T(8,128)} %scatter_fusion.1, s32[12]{0:T(128)S(1)} %fusion.64, f32[12,64,6,128]{3,1,2,0:T(8,128)S(1)} %convert_bitcast_fusion.2), kind=kCustom, calls=%fused_computation.25 | custom fusion | flops 589824 | bytes 7077984 | tf_op jit(solution)/shard_map/scatter-add | solution.py:140
  263.1 7.6 %convert_element_type.94 = bf16[3,64,32,6,128]{4,1,3,2,0:T(8,128)(2,1)S(1)} convert(f32[3,64,32,6,128]{4,1,3,2,0:T(8,128)} %scatter_fusion.2) | non-fusion elementwise | flops 4718592 | bytes 28311552 | tf_op jit(solution)/shard_map/convert_element_type | solution.py:143
  270.7 1.3 fusion.27
  272.1 1.3 fusion.26
  273.4 1.3 fusion.25
  274.7 1.3 fusion.24
  276.1 1.3 fusion.23
  277.4 1.3 fusion.22
  278.7 1.3 fusion.21
  280.1 1.3 fusion.20
  281.4 5.4 %all-to-all-start.1 = ((bf16[8,3,8,32,6,128]{5,2,4,3,1,0:T(8,128)(2,1)}), bf16[8,3,8,32,6,128]{5,2,4,3,1,0:T(8,128)(2,1)}, u32[]{:S(2)}, u32[]{:S(2)}) async-start(bf16[8,3,8,32,6,128]{5,2,4,3,1,0:T(8,128)(2,1)} %fusion.20), calls=%async_computation.1 | async-start | bytes 18874368 | tf_op jit(solution)/shard_map/all_to_all | solution.py:145
  286.8 25.0 %fusion.6 = f32[3,4,2,1536,128]{3,4,2,0,1:T(8,128)} fusion(bf16[4,1536,1536]{2,1,0:T(8,128)(2,1)} %param.6, bf16[3,4,2,1536,128]{4,3,2,1,0:T(8,128)(2,1)} %bitcast.208), kind=kOutput, calls=%fused_computation.35 | convolution fusion | flops 14495514624 | bytes 47185920 | tf_op jit(solution)/shard_map/hij,shpjx->shpix/dot_general | solution.py:153
  311.8 18.6 %copy.17 = f32[3,4,2,1536,128]{4,3,2,1,0:T(8,128)} copy(f32[3,4,2,1536,128]{3,4,2,0,1:T(8,128)} %fusion.6) | data formatting | bytes 37748736 | tf_op jit(solution)/shard_map/hij,shpjx->shpix/transpose | solution.py:153
  330.4 61.8 %all-to-all-done.1 = bf16[8,3,8,32,6,128]{5,2,4,3,1,0:T(8,128)(2,1)} async-done(((bf16[8,3,8,32,6,128]{5,2,4,3,1,0:T(8,128)(2,1)}), bf16[8,3,8,32,6,128]{5,2,4,3,1,0:T(8,128)(2,1)}, u32[]{:S(2)}, u32[]{:S(2)}) %all-to-all-start.1) | async-done | bytes 9437216 | tf_op jit(solution)/shard_map/all_to_all | solution.py:145
  392.2 12.4 %convert_bitcast_fusion = f32[3,8,32,8,6,128]{5,1,4,2,0,3:T(8,128)} fusion(bf16[8,3,8,32,6,128]{5,2,4,3,1,0:T(8,128)(2,1)} %all-to-all-done.1), kind=kLoop, calls=%fused_computation.30 | loop fusion | flops 4718592 | bytes 28311552 | tf_op jit(solution)/shard_map/convert_element_type | solution.py:154
  404.6 12.8 %copy.22 = f32[3,8,32,8,6,128]{5,2,4,3,1,0:T(8,128)S(1)} copy(f32[3,8,32,8,6,128]{5,1,4,2,0,3:T(8,128)} %convert_bitcast_fusion) | data formatting | bytes 37748736 | tf_op jit(solution)/shard_map/convert_element_type | solution.py:154
  417.4 13.1 %fusion.2 = bf16[3,8,32,48,128]{4,3,2,1,0:T(8,128)(2,1)} fusion(f32[3,8,32,48,128]{4,3,2,1,0:T(8,128)S(1)} %bitcast.206, f32[3,8,32,48,128]{4,2,3,1,0:T(8,128)S(1)} %bitcast.207), kind=kLoop, calls=%fused_computation.29 | loop fusion | flops 9437184 | bytes 47185920 | tf_op jit(solution)/shard_map/convert_element_type | solution.py:155
  (94 shorter events, 16.3 us)
Async XLA Ops:
  9.9 5.3 %copy-start.9 = (s32[4]{0:T(128)S(1)}, s32[4]{0:T(128)}, u32[]{:S(2)}) copy-start(s32[4]{0:T(128)} %param.9) | copy-start | bytes 52
  9.9 6.7 %copy-start.2 = (s32[72,3]{0,1:T(4,128)S(1)}, s32[72,3]{0,1:T(4,128)}, u32[]{:S(2)}) copy-start(s32[72,3]{0,1:T(4,128)} %param.8) | copy-start | bytes 2596
  9.9 111.2 %all-to-all-start = ((bf16[3,8,32,48,128]{4,2,1,0,3:T(8,128)(2,1)}), bf16[3,8,32,48,128]{4,2,1,0,3:T(8,128)(2,1)}, u32[]{:S(2)}, u32[]{:S(2)}) async-start(bf16[3,8,32,48,128]{4,2,1,0,3:T(8,128)(2,1)} %copy.19), calls=%async_computation | async-start | bytes 18874368 | tf_op jit(solution)/shard_map/all_to_all | solution.py:44
  32.5 88.6 %copy-start.4 = (pred[64]{0:T(512)(128)(4,1)}, pred[64]{0:T(512)(128)(4,1)S(1)}, u32[]{:S(2)}) copy-start(pred[64]{0:T(512)(128)(4,1)S(1)} %fusion.51) | copy-start | bytes 196
  32.6 88.5 %copy-start.7 = (s32[64]{0:T(128)}, s32[64]{0:T(128)S(1)}, u32[]{:S(2)}) copy-start(s32[64]{0:T(128)S(1)} %fusion.52) | copy-start | bytes 772
  133.2 15.2 %copy-start.3 = (f32[3,32,6]{1,2,0:T(8,128)S(1)}, f32[3,32,6]{1,2,0:T(8,128)}, u32[]{:S(2)}) copy-start(f32[3,32,6]{1,2,0:T(8,128)} %param.7) | copy-start | bytes 6916
  142.5 31.6 %collective-permute-start = (bf16[1,6,128,6,128]{4,2,3,1,0:T(8,128)(2,1)}, bf16[1,6,128,6,128]{4,2,3,1,0:T(8,128)(2,1)}, u32[]{:S(2)}, u32[]{:S(2)}) collective-permute-start(bf16[1,6,128,6,128]{4,2,3,1,0:T(8,128)(2,1)} %get-tuple-element.10), channel_id=1, source_target_pairs={{0,8},{8,16},{16,24},{24,0},{1,9},{9,17},{17,25},{25,1},{2,10},{10... | collective-permute-start | bytes 3538952 | tf_op jit(solution)/shard_map/ppermute | solution.py:17
  144.8 50.1 %collective-permute-start.1 = (bf16[1,6,128,6,128]{4,2,3,1,0:T(8,128)(2,1)}, bf16[1,6,128,6,128]{4,2,3,1,0:T(8,128)(2,1)}, u32[]{:S(2)}, u32[]{:S(2)}) collective-permute-start(bf16[1,6,128,6,128]{4,2,3,1,0:T(8,128)(2,1)} %get-tuple-element.11), channel_id=1, source_target_pairs={{8,0},{16,8},{24,16},{0,24},{9,1},{17,9},{25,17},{1,25},{10,2},{18... | collective-permute-start | bytes 3538952 | tf_op jit(solution)/shard_map/ppermute | solution.py:19
  194.9 8.2 %copy-start.10 = (s32[18,1]{0,1:T(1,128)S(1)}, s32[18,1]{0,1:T(1,128)}, u32[]{:S(2)}) copy-start(s32[18,1]{0,1:T(1,128)} %get-tuple-element.6) | copy-start | bytes 220
  194.9 8.2 %copy-start.11 = (s32[18,1]{0,1:T(1,128)S(1)}, s32[18,1]{0,1:T(1,128)}, u32[]{:S(2)}) copy-start(s32[18,1]{0,1:T(1,128)} %get-tuple-element.7) | copy-start | bytes 220
  194.9 8.2 %copy-start.5 = (pred[64]{0:T(512)(128)(4,1)S(1)}, pred[64]{0:T(512)(128)(4,1)}, u32[]{:S(2)}) copy-start(pred[64]{0:T(512)(128)(4,1)} %copy-done.4) | copy-start | bytes 196
  194.9 8.2 %copy-start.8 = (s32[64]{0:T(128)S(1)}, s32[64]{0:T(128)}, u32[]{:S(2)}) copy-start(s32[64]{0:T(128)} %copy-done.7) | copy-start | bytes 772
  200.7 29.7 %collective-permute-start.2 = (bf16[1,6,128,6,128]{4,2,3,1,0:T(8,128)(2,1)}, bf16[1,6,128,6,128]{4,2,3,1,0:T(8,128)(2,1)}, u32[]{:S(2)}, u32[]{:S(2)}) collective-permute-start(bf16[1,6,128,6,128]{4,2,3,1,0:T(8,128)(2,1)} %get-tuple-element.8), channel_id=1, source_target_pairs={{8,0},{16,8},{24,16},{0,24},{9,1},{17,9},{25,17},{1,25},{10,2},{18... | collective-permute-start | bytes 3538952 | tf_op jit(solution)/shard_map/ppermute | solution.py:19
  203.0 50.8 %collective-permute-start.3 = (bf16[1,6,128,6,128]{4,2,3,1,0:T(8,128)(2,1)}, bf16[1,6,128,6,128]{4,2,3,1,0:T(8,128)(2,1)}, u32[]{:S(2)}, u32[]{:S(2)}) collective-permute-start(bf16[1,6,128,6,128]{4,2,3,1,0:T(8,128)(2,1)} %get-tuple-element.9), channel_id=1, source_target_pairs={{0,8},{8,16},{16,24},{24,0},{1,9},{9,17},{17,25},{25,1},{2,10},{10... | collective-permute-start | bytes 3538952 | tf_op jit(solution)/shard_map/ppermute | solution.py:17
  214.1 11.5 %copy-start.1 = (s32[6]{0:T(128)S(1)}, s32[6]{0:T(128)}, u32[]{:S(2)}) copy-start(s32[6]{0:T(128)} %get-tuple-element.25) | copy-start | bytes 76
  214.1 39.8 %copy-start.6 = (pred[64]{0:T(512)(128)(4,1)S(1)}, pred[64]{0:T(512)(128)(4,1)}, u32[]{:S(2)}) copy-start(pred[64]{0:T(512)(128)(4,1)} %copy-done.4) | copy-start | bytes 196
  281.4 110.8 %all-to-all-start.1 = ((bf16[8,3,8,32,6,128]{5,2,4,3,1,0:T(8,128)(2,1)}), bf16[8,3,8,32,6,128]{5,2,4,3,1,0:T(8,128)(2,1)}, u32[]{:S(2)}, u32[]{:S(2)}) async-start(bf16[8,3,8,32,6,128]{5,2,4,3,1,0:T(8,128)(2,1)} %fusion.20), calls=%async_computation.1 | async-start | bytes 18874368 | tf_op jit(solution)/shard_map/all_to_all | solution.py:145
  404.6 12.8 %copy-start = (f32[3,4,2,1536,128]{4,3,2,1,0:T(8,128)S(1)}, f32[3,4,2,1536,128]{4,3,2,1,0:T(8,128)}, u32[]{:S(2)}) copy-start(f32[3,4,2,1536,128]{4,3,2,1,0:T(8,128)} %copy.17) | copy-start | bytes 56623108
